TPU v7x, 32 devices: a whole 2x2x4 slice. The times are simulated.
32 devices in a mesh: tm: 8 (over z, y), tensor: 4 (over x, core).
Axes of the slice: x: 2, y: 2, z: 4, core: 2. Of those that a mesh axis runs over, the one named last changes fastest.
Arguments:
- frames_in: bfloat16 [8, 1024, 768], P('tm'), may hold values from -16 to 16
- norm_gain: float32 [768], replicated, may hold values from 0.1 to 1.9
- w_qkv: bfloat16 [768, 3, 768], P(None, None, 'tensor'), may hold values from -0.21650635 to 0.21650635
- w_out: bfloat16 [768, 768], P('tensor'), may hold values from -0.21875 to 0.21875
- keep_runs: int32 [8, 16, 2], replicated, may hold values from 0 to 1023, as said below
- out_cotangent: bfloat16 [8, 1024, 768], P('tm'), may hold values from -6 to 6
Outputs:
- block_out: bfloat16 [8, 1024, 768], P('tm', None, 'tensor')
- grad_in: bfloat16 [8, 1024, 768], P('tm', None, 'tensor')
- grad_qkv: bfloat16 [768, 3, 768], P('tm', None, 'tensor')
- grad_proj: bfloat16 [768, 768], P('tensor', 'tm')
- grad_gain: float32 [768], P('tensor')
Inputs may be any that keep to these rules, and one draw needn't show every extreme that they name: keep_runs[t, r] = (first, length) is the r-th run of kept positions of frame t; the 16 runs of a frame are disjoint, in rising order, and lie within the frame's 1024 positions.
All inputs are finite; a program needn't handle non-finite values.
Results may differ from a plain program's by a relative error of at most 0.034.
Values may be sent and summed in bfloat16 or wider, within the bound.
No kernel may reach another device: no remote copies, remote signals or barrier semaphores. Data moves between devices by JAX's collectives and lax.ppermute only.
A program may use at most 128 MiB of HBM per device.

v0:
```python
import jax
import jax.numpy as jnp
from jax import lax
from jax.sharding import PartitionSpec as P

D = 768
H = 12
epsilon = 1e-05


def kept_table(keep_runs, first_place, place_count):
    places = first_place + jnp.arange(place_count, dtype=jnp.int32)
    starts = keep_runs[:, :, 0:1]
    lengths = keep_runs[:, :, 1:2]
    inside = (places[None, None, :] >= starts) & (places[None, None, :] < starts + lengths)
    return jnp.sum(inside.astype(jnp.int32), axis=1)


def normalize(frames_in):
    frames_float = frames_in.astype(jnp.float32)
    centre = jnp.mean(frames_float, axis=-1, keepdims=True)
    shifted = frames_float - centre
    spread = jnp.mean(shifted * shifted, axis=-1, keepdims=True)
    inverse_spread = lax.rsqrt(spread + epsilon)
    return (frames_float, shifted * inverse_spread, inverse_spread)


def attend(packed, kept_mask):
    frames, places, row_width = packed.shape
    head_width = D // H
    pieces = packed.reshape(frames, places, 3, row_width // (3 * head_width), head_width)
    scores = jnp.einsum(
        "tphd,uphd->phtu", pieces[:, :, 0], pieces[:, :, 1], preferred_element_type=jnp.float32
    )
    scores = scores * head_width ** (-0.5)
    allowed = jnp.transpose(kept_mask)[:, None, None, :] > 0
    scores = jnp.where(allowed, scores, -1000000000.0)
    row_max = jnp.max(scores, axis=-1, keepdims=True)
    exponent = jnp.exp(scores - row_max)
    weights = (exponent / jnp.sum(exponent, axis=-1, keepdims=True)).astype(jnp.bfloat16)
    mixed_rows = jnp.einsum(
        "phtu,uphd->tphd", weights, pieces[:, :, 2], preferred_element_type=jnp.float32
    )
    mixed_rows = jnp.where(kept_mask[:, :, None, None] > 0, mixed_rows, 0.0)
    return mixed_rows.astype(jnp.bfloat16).reshape(frames, places, row_width // 3)


def project(rows_in, weight):
    leading = rows_in.shape[:-1]
    flat = jnp.dot(
        rows_in.reshape(-1, rows_in.shape[-1]), weight, preferred_element_type=jnp.float32
    )
    return flat.astype(jnp.bfloat16).reshape(leading + (weight.shape[1],))


def contract_rows(left, right):
    return lax.dot_general(
        left.reshape(-1, left.shape[-1]),
        right.reshape(-1, right.shape[-1]),
        (((0,), (0,)), ((), ())),
        preferred_element_type=jnp.float32,
    )


def back_project(cotangent, weight):
    leading = cotangent.shape[:-1]
    flat = lax.dot_general(
        cotangent.reshape(-1, cotangent.shape[-1]),
        weight,
        (((1,), (1,)), ((), ())),
        preferred_element_type=jnp.float32,
    )
    return flat.reshape(leading + (weight.shape[0],))


def body(frames_in, norm_gain, w_qkv, w_out, keep_runs, out_cotangent):
    frames_here, place_total, row_width = frames_in.shape
    places_here = place_total // lax.axis_size("tm")
    width_share = row_width // lax.axis_size("tensor")
    share_start = lax.axis_index("tensor") * width_share
    channels = w_qkv.shape[2]
    w_flat = w_qkv.reshape(row_width, 3 * channels)
    kept_mask = kept_table(keep_runs, lax.axis_index("tm") * places_here, places_here)
    frames_float, standard, inverse_spread = normalize(frames_in)
    normed = (standard * norm_gain).astype(jnp.bfloat16)
    packed = project(normed, w_flat)
    packed_places = lax.all_to_all(packed, "tm", split_axis=1, concat_axis=0, tiled=True)

    def attend_here(packed_arg):
        return attend(packed_arg, kept_mask)

    mixed_places, attend_back = jax.vjp(attend_here, packed_places)
    mixed_frames = lax.all_to_all(mixed_places, "tm", split_axis=0, concat_axis=1, tiled=True)
    branch = jnp.dot(mixed_frames.reshape(-1, channels), w_out, preferred_element_type=jnp.float32)
    branch = branch.reshape(frames_here, place_total, row_width)
    branch_share = lax.psum_scatter(
        branch.astype(jnp.bfloat16), "tensor", scatter_dimension=2, tiled=True
    ).astype(jnp.float32)
    residual_share = lax.dynamic_slice_in_dim(frames_float, share_start, width_share, 2)
    block_out = (residual_share + branch_share).astype(jnp.bfloat16)
    proj_part = contract_rows(mixed_frames, out_cotangent)
    grad_proj = lax.psum_scatter(proj_part, "tm", scatter_dimension=1, tiled=True).astype(
        jnp.bfloat16
    )
    mixed_cot = back_project(out_cotangent, w_out).astype(jnp.bfloat16)
    mixed_cot_places = lax.all_to_all(mixed_cot, "tm", split_axis=1, concat_axis=0, tiled=True)
    packed_cot_places = attend_back(mixed_cot_places)[0]
    gain_share = lax.dynamic_slice_in_dim(norm_gain, share_start, width_share, 0)
    standard_share = lax.dynamic_slice_in_dim(standard, share_start, width_share, 2)
    packed_cot = lax.all_to_all(packed_cot_places, "tm", split_axis=0, concat_axis=1, tiled=True)
    qkv_part = contract_rows(normed, packed_cot)
    normed_part = back_project(packed_cot, w_flat)
    whole_cot = lax.psum(normed_part.astype(jnp.bfloat16), "tensor").astype(jnp.float32)
    whole_cot = lax.optimization_barrier(whole_cot.astype(jnp.bfloat16)).astype(jnp.float32)
    scaled_whole = whole_cot * norm_gain
    mean_plain = jnp.mean(scaled_whole, axis=-1, keepdims=True)
    mean_cross = jnp.mean(scaled_whole * standard, axis=-1, keepdims=True)
    cot_share = lax.dynamic_slice_in_dim(whole_cot, share_start, width_share, 2)
    scaled_share = cot_share * gain_share
    through = inverse_spread * (scaled_share - mean_plain - standard_share * mean_cross)
    gain_part = jnp.sum(cot_share * standard_share, axis=(0, 1))
    cot_share_out = lax.dynamic_slice_in_dim(out_cotangent, share_start, width_share, 2).astype(
        jnp.float32
    )
    grad_in = (cot_share_out + through).astype(jnp.bfloat16)
    grad_qkv = lax.psum_scatter(
        qkv_part.reshape(row_width, 3, channels), "tm", scatter_dimension=0, tiled=True
    ).astype(jnp.bfloat16)
    grad_gain = lax.psum(gain_part, "tm")
    return (block_out, grad_in, grad_qkv, grad_proj, grad_gain)


def solution(mesh):
    in_specs = (
        P("tm", None, None),
        P(),
        P(None, None, "tensor"),
        P("tensor", None),
        P(),
        P("tm", None, None),
    )
    out_specs = (
        P("tm", None, "tensor"),
        P("tm", None, "tensor"),
        P("tm", None, "tensor"),
        P("tensor", "tm"),
        P("tensor"),
    )
    return jax.shard_map(body, mesh=mesh, in_specs=in_specs, out_specs=out_specs, check_vma=False)
```

profile of v0, /device:TPU:0, one launch (start us, length us, event | category | flops | bytes accessed | tf_op | source)
XLA Modules:
  0.0 338.7 jit_solution(6467486779215469923)
XLA Ops:
  8.0 2.2 fusion.29
  10.2 0.8 copy.115
  11.0 0.5 broadcast.97
  11.6 4.9 %reduce.4 = bf16[1024,192]{1,0:T(8,128)(2,1)} reduce(bf16[1024,1,192]{2,1,0:T(2,128)(2,1)S(1)} %bitcast.147, bf16[]{:T(256)} %broadcast.97), dimensions={1}, to_apply=%bitcast.110.reduce_sub_computation | reduce | bytes 786434
  16.5 2.4 reshape.160
  18.9 7.7 %all-to-all-start.2 = ((bf16[8,2,12288]{2,1,0:T(2,128)(2,1)}), bf16[8,2,12288]{2,1,0:T(2,128)(2,1)S(1)}, u32[]{:S(2)}, u32[]{:S(2)}) async-start(bf16[8,2,12288]{2,1,0:T(2,128)(2,1)} %reshape.160), calls=%async_computation.2 | async-start | bytes 786432 | tf_op jit(solution)/shard_map/all_to_all | solution.py:106
  27.0 0.6 multiply_reduce_fusion.1
  27.6 2.3 fusion.17
  29.9 6.2 %copy.106 = bf16[1,1024,576]{2,0,1:T(2,128)(2,1)} copy(bf16[1,1024,576]{1,2,0:T(8,128)(2,1)} %fusion.17) | data formatting | bytes 2359296 | tf_op jit(solution)/shard_map/reshape | solution.py:53
  36.1 11.0 %reduce.5 = bf16[1024,576]{1,0:T(8,128)(2,1)} reduce(bf16[1024,1,576]{2,1,0:T(2,128)(2,1)} %bitcast.141, bf16[]{:T(256)} %broadcast.97), dimensions={1}, to_apply=%bitcast.108.reduce_sub_computation | reduce | bytes 2359298
  47.1 4.4 %reshape.158 = bf16[8,2,36864]{2,1,0:T(2,128)(2,1)} reshape(bf16[1024,576]{1,0:T(8,128)(2,1)} %reduce.5) | data formatting | bytes 2359296
  51.5 17.1 %all-to-all-start = ((bf16[8,2,36864]{2,1,0:T(2,128)(2,1)}), bf16[8,2,36864]{2,1,0:T(2,128)(2,1)}, u32[]{:S(2)}, u32[]{:S(2)}) async-start(bf16[8,2,36864]{2,1,0:T(2,128)(2,1)} %reshape.158), calls=%async_computation | async-start | bytes 2359296 | tf_op jit(solution)/shard_map/all_to_all | solution.py:87
  69.0 2.4 reshape.161
  71.4 1.7 copy.116
  73.1 1.8 copy.143
  74.9 22.0 %all-to-all-done = bf16[8,2,36864]{2,1,0:T(2,128)(2,1)} async-done(((bf16[8,2,36864]{2,1,0:T(2,128)(2,1)}), bf16[8,2,36864]{2,1,0:T(2,128)(2,1)}, u32[]{:S(2)}, u32[]{:S(2)}) %all-to-all-start) | async-done | bytes 1179680 | tf_op jit(solution)/shard_map/all_to_all | solution.py:87
  96.9 6.5 %reshape.159 = bf16[1024,1,576]{2,1,0:T(2,128)(2,1)} reshape(bf16[8,2,36864]{2,1,0:T(2,128)(2,1)} %all-to-all-done) | data formatting | bytes 2359296
  103.4 6.0 %copy.107 = bf16[1,1024,576]{1,2,0:T(8,128)(2,1)} copy(bf16[1,1024,576]{2,0,1:T(2,128)(2,1)} %bitcast.142) | data formatting | bytes 2359296 | tf_op jit(solution)/shard_map/all_to_all | solution.py:87
  109.4 1.6 copy.142
  111.0 1.0 fusion.60
  112.0 1.6 copy.138
  113.6 2.7 copy.137
  116.3 2.4 copy.139
  118.7 2.0 fusion.62
  120.8 0.7 fusion.32
  121.5 0.8 multiply_divide_fusion
  122.5 1.6 fusion.39
  124.0 2.3 copy.113
  126.3 2.1 fusion.41
  128.4 3.5 %all-to-all-start.1 = ((bf16[8,128,192]{1,2,0:T(8,128)(2,1)}), bf16[8,128,192]{1,2,0:T(8,128)(2,1)S(1)}, u32[]{:S(2)}, u32[]{:S(2)}) async-start(bf16[8,128,192]{1,2,0:T(8,128)(2,1)} %bitcast.149), calls=%async_computation.1 | async-start | bytes 786432 | tf_op jit(solution)/shard_map/all_to_all | solution.py:93
  131.9 2.2 copy.118
  134.1 3.7 %convert_reduce_fusion.1 = (f32[128,3,8]{2,1,0:T(4,128)S(1)}, pred[128,3,8,8]{2,3,1,0:T(8,128)(4,1)S(1)}, f32[128,3,8]{2,1,0:T(4,128)S(1)}, bf16[128,3,8,8]{2,3,1,0:T(8,128)(2,1)S(1)}) fusion(f32[128,3,8,8]{2,3,1,0:T(8,128)} %copy-done.2, f32[128,3,8]{2,1,0:T(4,128)S(1)} %get-tuple-element.57, f32[128,3,8]{2,1,0:T(4,128)} %multiply_divide_fusion, ...), kind=kOutput, calls=%fused_computation.25 | convolution fusion | flops 3336192 | bytes 1007616 | tf_op jit(solution)/shard_map/transpose(jvp(phtu,uphd->tphd))/dot_general | solution.py:41
  137.9 1.0 fusion.58
  139.0 1.0 fusion.22
  140.2 0.7 fusion.21
  140.8 0.5 copy-done.12
  141.3 0.6 fusion.20
  141.9 2.0 pad_add_fusion
  143.9 4.0 %copy.121 = bf16[8,128,3,3,64]{1,4,3,2,0:T(8,128)(2,1)} copy(bf16[8,128,3,3,64]{4,0,3,1,2:T(8,128)(2,1)} %pad_add_fusion) | data formatting | bytes 2359296 | tf_op jit(solution)/shard_map/transpose(jvp())/add_any | solution.py:33
  147.9 6.0 %all-to-all-start.3 = ((bf16[8,128,576]{1,2,0:T(8,128)(2,1)}), bf16[8,128,576]{1,2,0:T(8,128)(2,1)}, u32[]{:S(2)}, u32[]{:S(2)}) async-start(bf16[8,128,576]{1,2,0:T(8,128)(2,1)} %bitcast.144), calls=%async_computation.3 | async-start | bytes 2359296 | tf_op jit(solution)/shard_map/all_to_all | solution.py:110
  153.9 3.0 fusion.23
  157.0 28.6 %all-to-all-done.3 = bf16[8,128,576]{1,2,0:T(8,128)(2,1)} async-done(((bf16[8,128,576]{1,2,0:T(8,128)(2,1)}), bf16[8,128,576]{1,2,0:T(8,128)(2,1)}, u32[]{:S(2)}, u32[]{:S(2)}) %all-to-all-start.3) | async-done | bytes 1179680 | tf_op jit(solution)/shard_map/all_to_all | solution.py:110
  185.6 3.9 %fusion.16 = bf16[1,1024,768]{2,1,0:T(8,128)(2,1)} fusion(bf16[768,576]{0,1:T(8,128)(2,1)S(1)} %bitcast.139, bf16[8,128,576]{1,2,0:T(8,128)(2,1)} %all-to-all-done.3), kind=kOutput, calls=%fused_computation.31 | convolution fusion | flops 906756096 | bytes 3637248 | tf_op jit(solution)/shard_map/dot_general | solution.py:67
  189.6 0.9 copy-done.10
  190.5 1.8 fusion.15
  192.2 8.5 %copy.130 = bf16[1,1024,768]{1,0,2:T(2,128)(2,1)} copy(bf16[1,1024,768]{2,1,0:T(8,128)(2,1)} %fusion.15) | data formatting | bytes 3145728
  200.7 3.7 %copy.158 = bf16[768,1,1024]{2,0,1:T(8,128)(2,1)} copy(bf16[768,1,1024]{2,1,0:T(2,128)(2,1)} %bitcast.140) | data formatting | bytes 3145728
  204.7 1.4 copy_bitcast_fusion.1
  206.1 3.3 fusion.4
  209.4 1.9 convert_element_type.92
  211.4 15.4 %reduce-scatter.12.cloned.1.call-done = f32[96,192]{1,0:T(8,128)} async-done(((f32[768,192]{1,0:T(8,128)}), f32[96,192]{1,0:T(8,128)}) %reduce-scatter.12.cloned.1.call-update) | async-done | bytes 73744
  226.8 1.6 copy.133
  228.4 3.5 %all-reduce.5.cloned.1.call-done = bf16[1,1024,768]{2,1,0:T(8,128)(2,1)} async-done(((bf16[1,1024,768]{2,1,0:T(8,128)(2,1)}), bf16[1,1024,768]{2,1,0:T(8,128)(2,1)}) %all-reduce.5.cloned.1.call-update) | async-done | bytes 1572880 | tf_op jit(solution)/shard_map/psum | solution.py:113
  232.0 1.8 convert_element_type.118
  233.9 1.2 multiply_reduce_fusion.2
  235.1 2.5 multiply_reduce_fusion.3
  237.6 0.9 copy.125
  238.5 21.8 %psum.15 = f32[192]{0:T(256)} all-reduce(f32[192]{0:T(256)S(1)} %get-tuple-element.46), channel_id=1, replica_groups=mesh['tm'=8,'tensor'=4] {'tm'}, use_global_device_ids=true, to_apply=%region_15.16 | all-reduce | flops 192 | bytes 1536 | tf_op jit(solution)/shard_map/psum | solution.py:129
  260.4 1.4 reshape_bitcast_fusion
  261.8 1.1 copy.131
  262.9 1.8 add_convert_fusion.1
  264.7 0.9 copy.124
  265.6 64.1 %reduce-scatter.8.cloned.1.call-done = f32[96,3,192]{2,0,1:T(8,128)} async-done(((f32[768,3,192]{2,0,1:T(8,128)}), f32[96,3,192]{2,0,1:T(8,128)}) %reduce-scatter.8.cloned.1.call-update) | async-done | bytes 221200 | tf_op jit(solution)/shard_map/reduce_scatter | solution.py:126
  329.7 1.6 convert_element_type.120
  (53 shorter events, 1.8 us)
Async XLA Ops:
  8.0 19.6 %copy-start = (bf16[768,3,192]{0,2,1:T(8,128)(2,1)S(1)}, bf16[768,3,192]{0,2,1:T(8,128)(2,1)}, u32[]{:S(2)}) copy-start(bf16[768,3,192]{0,2,1:T(8,128)(2,1)} %param.8) | copy-start | bytes 2654212
  11.6 15.1 %copy-start.1 = (bf16[1,1024,768]{2,1,0:T(8,128)(2,1)S(1)}, bf16[1,1024,768]{2,1,0:T(8,128)(2,1)}, u32[]{:S(2)}) copy-start(bf16[1,1024,768]{2,1,0:T(8,128)(2,1)} %param.6) | copy-start | bytes 4718596
  18.9 32.6 %all-to-all-start.2 = ((bf16[8,2,12288]{2,1,0:T(2,128)(2,1)}), bf16[8,2,12288]{2,1,0:T(2,128)(2,1)S(1)}, u32[]{:S(2)}, u32[]{:S(2)}) async-start(bf16[8,2,12288]{2,1,0:T(2,128)(2,1)} %reshape.160), calls=%async_computation.2 | async-start | bytes 786432 | tf_op jit(solution)/shard_map/all_to_all | solution.py:106
  26.7 0.9 copy-start.14
  51.5 17.2 %copy-start.13 = (s32[8,16,2]{1,2,0:T(2,128)S(1)}, s32[8,16,2]{1,2,0:T(2,128)}, u32[]{:S(2)}) copy-start(s32[8,16,2]{1,2,0:T(2,128)} %param.10) | copy-start | bytes 3076
  51.5 17.5 %copy-start.8 = (bf16[8,2,12288]{2,1,0:T(2,128)(2,1)}, bf16[8,2,12288]{2,1,0:T(2,128)(2,1)S(1)}, u32[]{:S(2)}) copy-start(bf16[8,2,12288]{2,1,0:T(2,128)(2,1)S(1)} %all-to-all-done.2) | copy-start | bytes 1179652
  51.5 45.4 %all-to-all-start = ((bf16[8,2,36864]{2,1,0:T(2,128)(2,1)}), bf16[8,2,36864]{2,1,0:T(2,128)(2,1)}, u32[]{:S(2)}, u32[]{:S(2)}) async-start(bf16[8,2,36864]{2,1,0:T(2,128)(2,1)} %reshape.158), calls=%async_computation | async-start | bytes 2359296 | tf_op jit(solution)/shard_map/all_to_all | solution.py:87
  113.6 7.1 %copy-start.5 = (bf16[8,128,1,3,64]{4,0,3,1,2:T(8,128)(2,1)}, bf16[8,128,1,3,64]{4,0,3,1,2:T(8,128)(2,1)S(1)}, u32[]{:S(2)}) copy-start(bf16[8,128,1,3,64]{4,0,3,1,2:T(8,128)(2,1)S(1)} %copy.138) | copy-start | bytes 1179652
  120.7 1.5 copy-start.2
  120.7 1.7 copy-start.11
  122.4 3.9 %copy-start.9 = (bf16[24,8,8,128]{3,2,1,0:T(8,128)(2,1)S(1)}, bf16[24,8,8,128]{3,2,1,0:T(8,128)(2,1)}, u32[]{:S(2)}) copy-start(bf16[24,8,8,128]{3,2,1,0:T(8,128)(2,1)} %copy.143) | copy-start | bytes 1179652
  128.4 19.5 %all-to-all-start.1 = ((bf16[8,128,192]{1,2,0:T(8,128)(2,1)}), bf16[8,128,192]{1,2,0:T(8,128)(2,1)S(1)}, u32[]{:S(2)}, u32[]{:S(2)}) async-start(bf16[8,128,192]{1,2,0:T(8,128)(2,1)} %bitcast.149), calls=%async_computation.1 | async-start | bytes 786432 | tf_op jit(solution)/shard_map/all_to_all | solution.py:93
  134.1 3.8 %copy-start.3 = (f32[128,3,8,8]{2,3,1,0:T(8,128)S(1)}, f32[128,3,8,8]{2,3,1,0:T(8,128)}, u32[]{:S(2)}) copy-start(f32[128,3,8,8]{2,3,1,0:T(8,128)} %copy-done.2) | copy-start | bytes 294916
  137.9 1.1 copy-start.7
  139.0 1.1 copy-start.6
  140.2 1.1 copy-start.12
  147.9 37.7 %all-to-all-start.3 = ((bf16[8,128,576]{1,2,0:T(8,128)(2,1)}), bf16[8,128,576]{1,2,0:T(8,128)(2,1)}, u32[]{:S(2)}, u32[]{:S(2)}) async-start(bf16[8,128,576]{1,2,0:T(8,128)(2,1)} %bitcast.144), calls=%async_computation.3 | async-start | bytes 2359296 | tf_op jit(solution)/shard_map/all_to_all | solution.py:110
  153.9 72.9 %reduce-scatter.12.cloned.1.call-start = ((), (), s32[]{:S(2)}) async-start(), calls=%async_computation.10 | async-start | bytes 884736
  157.0 75.0 %all-reduce.5.cloned.1.call-start = ((), (), s32[]{:S(2)}) async-start(), calls=%async_computation.7 | async-start | bytes 3145728 | tf_op jit(solution)/shard_map/psum | solution.py:113
  189.5 1.0 copy-start.10
  189.5 70.8 %reduce-scatter.10.cloned.1.call-start = ((), (), s32[]{:S(2)}) async-start(), calls=%async_computation.9 | async-start | bytes 1966080
  204.4 125.2 %reduce-scatter.8.cloned.1.call-start = ((), (), s32[]{:S(2)}) async-start(), calls=%async_computation.8 | async-start | bytes 2654208 | tf_op jit(solution)/shard_map/reduce_scatter | solution.py:126
  232.0 2.0 copy-start.4
Sparse Core Ops, SparseCore 0:
  158.0 68.7 reduce-scatter.11
  229.4 27.0 reduce-scatter.9
  260.0 69.6 reduce-scatter.7
Sparse Core Ops, SparseCore 1:
  189.6 42.3 all-reduce.4
where the time goes:
time: 345 us; the launch traced here: 339 us
  waiting for transfers between devices  134 us (39%)
  local copies, waits for them, and re-layouts  72.4 us (21%)
  starting transfers between devices  34.6 us (10%)
  other arithmetic  34.4 us (10%)
  matrix products  25.9 us (8%)
  blocking collectives  21.8 us (6%)
  between operations  15.8 us (5%)
    reduce_scatter x1, waiting for transfers between devices, body(): lax.psum_scatter(qkv_part.reshape(row_width, 3, channels), 'tm', scatter_...  64.1 us
    unnamed x47, local copies, waits for them, and re-layouts  46.5 us
    all_to_all x1, waiting for transfers between devices, body(): lax.all_to_all(packed_cot_places, 'tm', split_axis=0, concat_axis=1, tile...  28.6 us
    all_to_all x1, waiting for transfers between devices, body(): lax.all_to_all(packed, 'tm', split_axis=1, concat_axis=0, tiled=True)  22 us
    psum x1, blocking collectives, body(): grad_gain = lax.psum(gain_part, 'tm')  21.8 us
    all_to_all x1, starting transfers between devices, body(): lax.all_to_all(packed, 'tm', split_axis=1, concat_axis=0, tiled=True)  17.1 us
    unnamed x2, other arithmetic  16 us
    unnamed x6, waiting for transfers between devices  15.5 us
  transfers between devices with their start and end apart: 8, of which 5 were waited for; matrix products, arithmetic and copies ran while one was open for 26% of the time, Pallas kernels for 0%

commit v1 on v0

--- a/solution.py
+++ b/solution.py
@@ -84,7 +84,20 @@
     frames_float, standard, inverse_spread = normalize(frames_in)
     normed = (standard * norm_gain).astype(jnp.bfloat16)
     packed = project(normed, w_flat)
-    packed_places = lax.all_to_all(packed, "tm", split_axis=1, concat_axis=0, tiled=True)
+    ways, here = (lax.axis_size("tm"), lax.axis_index("tm"))
+    width = packed.shape[1] // ways
+    dims = list(packed.shape)
+    dims[1] = width
+    height = dims[0]
+    dims[0] = height * ways
+    packed_places = jnp.zeros(dims, packed.dtype)
+    for mask in range(ways):
+        part = lax.dynamic_slice_in_dim(packed, (here ^ mask) * width, width, axis=1)
+        if mask:
+            part = lax.ppermute(part, "tm", [(d, d ^ mask) for d in range(ways)])
+        packed_places = lax.dynamic_update_slice_in_dim(
+            packed_places, part, (here ^ mask) * height, axis=0
+        )
 
     def attend_here(packed_arg):
         return attend(packed_arg, kept_mask)

time: 345 us -> 305 us (0.88); the launches traced: 339 us -> 303 us
  waiting for transfers between devices: 134 us -> 121 us
  local copies, waits for them, and re-layouts: 72.4 us -> 60.1 us
  other arithmetic: 34.4 us -> 23.3 us
    all_to_all x1 -> x0, waiting for transfers between devices: 22 us -> none  [body(): lax.all_to_all(packed, 'tm', split_axis=1, concat_axis=0, tiled=True)]
    all_to_all x1 -> x0, starting transfers between devices: 17.1 us -> none  [body(): lax.all_to_all(packed, 'tm', split_axis=1, concat_axis=0, tiled=True)]
    ppermute x0 -> x7, starting transfers between devices: none -> 16.3 us  [body(): part = lax.ppermute(part, 'tm', [(d, d ^ mask) for d in range(ways)])]
    unnamed x47 -> x50, local copies, waits for them, and re-layouts: 46.5 us -> 33.8 us
    unnamed x2 -> x1, other arithmetic: 16 us -> 4.94 us
    dynamic_update_slice x0 -> x8, local copies, waits for them, and re-layouts: none -> 10.8 us  [body(): lax.dynamic_update_slice_in_dim(packed_places, part, (here ^ mask) * heig...]
    ppermute x0 -> x7, waiting for transfers between devices: none -> 10.2 us  [body(): part = lax.ppermute(part, 'tm', [(d, d ^ mask) for d in range(ways)])]
    reshape x1 -> x0, local copies, waits for them, and re-layouts: 6.18 us -> none  [project(): return flat.astype(jnp.bfloat16).reshape(leading + (weight.shape[1],))]
  transfers between devices with their start and end apart: 8 -> 14, of which waited for: 5 -> 6; matrix products, arithmetic and copies ran while one was open for 26% -> 28% of each run, Pallas kernels for 0% -> 0%
where the time goes in v1:
time: 305 us; the launch traced here: 303 us
  waiting for transfers between devices  121 us (40%)
  local copies, waits for them, and re-layouts  60.1 us (20%)
  starting transfers between devices  34.3 us (11%)
  matrix products  26.5 us (9%)
  other arithmetic  23.3 us (8%)
  blocking collectives  21.7 us (7%)
  between operations  15.6 us (5%)
    reduce_scatter x1, waiting for transfers between devices, body(): lax.psum_scatter(qkv_part.reshape(row_width, 3, channels), 'tm', scatter_...  63.9 us
    unnamed x50, local copies, waits for them, and re-layouts  33.8 us
    all_to_all x1, waiting for transfers between devices, body(): lax.all_to_all(packed_cot_places, 'tm', split_axis=0, concat_axis=1, tile...  28.7 us
    psum x1, blocking collectives, body(): grad_gain = lax.psum(gain_part, 'tm')  21.7 us
    ppermute x7, starting transfers between devices, body(): part = lax.ppermute(part, 'tm', [(d, d ^ mask) for d in range(ways)])  16.3 us
    unnamed x6, waiting for transfers between devices  14.8 us
    dynamic_update_slice x8, local copies, waits for them, and re-layouts, body(): lax.dynamic_update_slice_in_dim(packed_places, part, (here ^ mask) * heig...  10.8 us
    ppermute x7, waiting for transfers between devices, body(): part = lax.ppermute(part, 'tm', [(d, d ^ mask) for d in range(ways)])  10.2 us
  transfers between devices with their start and end apart: 14, of which 6 were waited for; matrix products, arithmetic and copies ran while one was open for 28% of the time, Pallas kernels for 0%

profile of v1, /device:TPU:0, one launch (start us, length us, event | category | flops | bytes accessed | tf_op | source)
XLA Modules:
  0.0 303.0 jit_solution(10116686517193640591)
XLA Ops:
  8.0 2.2 fusion.26
  10.2 0.8 copy.91
  11.6 4.9 %reduce.4 = bf16[1024,192]{1,0:T(8,128)(2,1)} reduce(bf16[1024,1,192]{2,1,0:T(2,128)(2,1)S(1)} %bitcast.148, bf16[]{:T(256)} %broadcast.97), dimensions={1}, to_apply=%bitcast.115.reduce_sub_computation | reduce | bytes 786434
  16.5 2.4 reshape.159
  18.9 7.3 %all-to-all-start.1 = ((bf16[8,2,12288]{2,1,0:T(2,128)(2,1)}), bf16[8,2,12288]{2,1,0:T(2,128)(2,1)}, u32[]{:S(2)}, u32[]{:S(2)}) async-start(bf16[8,2,12288]{2,1,0:T(2,128)(2,1)} %reshape.159), calls=%async_computation.1 | async-start | bytes 786432 | tf_op jit(solution)/shard_map/all_to_all | solution.py:119
  27.2 1.3 fusion.12
  28.5 1.0 copy-done.14
  29.8 4.8 %collective-permute-start.6 = (bf16[1,128,576]{1,2,0:T(8,128)(2,1)S(1)}, bf16[1,128,576]{1,2,0:T(8,128)(2,1)}, u32[]{:S(2)}, u32[]{:S(2)}) collective-permute-start(bf16[1,128,576]{1,2,0:T(8,128)(2,1)S(1)} %get-tuple-element.48), channel_id=1, source_target_pairs={{0,28},{4,24},{8,20},{12,16},{16,12},{20,8},{24,4},{28,0},{1,29},{... | collective-permute-start | bytes 442376 | tf_op jit(solution)/shard_map/ppermute | solution.py:97
  35.7 3.3 %collective-permute-start.1 = (bf16[1,128,576]{1,2,0:T(8,128)(2,1)S(1)}, bf16[1,128,576]{1,2,0:T(8,128)(2,1)}, u32[]{:S(2)}, u32[]{:S(2)}) collective-permute-start(bf16[1,128,576]{1,2,0:T(8,128)(2,1)S(1)} %get-tuple-element.53), channel_id=1, source_target_pairs={{0,8},{4,12},{8,0},{12,4},{16,24},{20,28},{24,16},{28,20},{1,9},{5... | collective-permute-start | bytes 442376 | tf_op jit(solution)/shard_map/ppermute | solution.py:97
  38.9 1.5 collective-permute-start
  40.6 1.2 broadcast_in_dim.63
  41.8 1.6 bitcast_dynamic-update-slice_fusion
  44.2 3.4 %collective-permute-start.2 = (bf16[1,128,576]{1,2,0:T(8,128)(2,1)S(1)}, bf16[1,128,576]{1,2,0:T(8,128)(2,1)S(1)}, u32[]{:S(2)}, u32[]{:S(2)}) collective-permute-start(bf16[1,128,576]{1,2,0:T(8,128)(2,1)S(1)} %get-tuple-element.52), channel_id=1, source_target_pairs={{0,12},{4,8},{8,4},{12,0},{16,28},{20,24},{24,20},{28,16},{1,13},{... | collective-permute-start | bytes 442376 | tf_op jit(solution)/shard_map/ppermute | solution.py:97
  47.6 1.6 constant_dynamic-update-slice_fusion.6
  49.2 2.3 collective-permute-start.3
  51.5 1.6 constant_dynamic-update-slice_fusion.5
  53.7 9.5 %collective-permute-done.3 = bf16[1,128,576]{1,2,0:T(8,128)(2,1)S(1)} collective-permute-done((bf16[1,128,576]{1,2,0:T(8,128)(2,1)S(1)}, bf16[1,128,576]{1,2,0:T(8,128)(2,1)S(1)}, u32[]{:S(2)}, u32[]{:S(2)}) %collective-permute-start.3) | collective-permute-done | bytes 147488 | tf_op jit(solution)/shard_map/ppermute | solution.py:97
  63.9 1.6 constant_dynamic-update-slice_fusion.2
  65.4 1.6 constant_dynamic-update-slice_fusion.1
  67.0 1.6 constant_dynamic-update-slice_fusion
  68.6 2.3 fusion.57
  70.9 1.4 copy.114
  72.3 2.5 copy.115
  74.8 2.0 fusion.59
  76.9 1.1 copy-done.2
  78.7 1.3 copy.113
  80.0 3.2 %fusion.36 = bf16[128,3,64,8]{2,3,1,0:T(8,128)(2,1)} fusion(bf16[8,128,1,3,64]{4,0,3,1,2:T(8,128)(2,1)} %copy.113, f32[128,3,8,8]{2,3,1,0:T(8,128)} %copy-done.2, f32[128,3,8]{2,1,0:T(4,128)S(1)} %fusion.29, f32[128,3,8]{2,1,0:T(4,128)S(1)} %get-tuple-element.59), kind=kOutput, calls=%fused_computation.55 | convolution fusion | flops 3219456 | bytes 909312 | tf_op jit(solution)/shard_map/jvp(phtu,uphd->tphd)/dot_general | solution.py:41
  83.2 2.3 copy.89
  86.2 2.3 reshape.160
  88.6 1.7 copy.92
  90.4 1.1 copy.118
  91.4 2.0 fusion.38
  93.4 4.3 %all-to-all-start = ((bf16[8,128,192]{1,2,0:T(8,128)(2,1)}), bf16[8,128,192]{1,2,0:T(8,128)(2,1)S(1)}, u32[]{:S(2)}, u32[]{:S(2)}) async-start(bf16[8,128,192]{1,2,0:T(8,128)(2,1)} %bitcast.18), calls=%async_computation | async-start | bytes 786432 | tf_op jit(solution)/shard_map/all_to_all | solution.py:106
  97.7 1.2 copy.94
  99.0 3.7 %convert_reduce_fusion.1 = (f32[128,3,8]{2,1,0:T(4,128)S(1)}, pred[128,3,8,8]{2,3,1,0:T(8,128)(4,1)S(1)}, f32[128,3,8]{2,1,0:T(4,128)S(1)}, bf16[128,3,8,8]{2,3,1,0:T(8,128)(2,1)S(1)}) fusion(f32[128,3,8,8]{2,3,1,0:T(8,128)} %copy-done.2, f32[128,3,8]{2,1,0:T(4,128)S(1)} %copy-done.11, f32[128,3,8]{2,1,0:T(4,128)} %multiply_divide_fusion, ...), kind=kOutput, calls=%fused_computation.25 | convolution fusion | flops 3336192 | bytes 1007616 | tf_op jit(solution)/shard_map/transpose(jvp(phtu,uphd->tphd))/dot_general | solution.py:41
  102.8 1.0 fusion.55
  103.9 1.0 fusion.19
  106.8 2.0 pad_add_fusion
  108.8 4.0 %copy.97 = bf16[8,128,3,3,64]{1,4,3,2,0:T(8,128)(2,1)} copy(bf16[8,128,3,3,64]{4,0,3,1,2:T(8,128)(2,1)} %pad_add_fusion) | data formatting | bytes 2359296 | tf_op jit(solution)/shard_map/transpose(jvp())/add_any | solution.py:33
  112.8 6.0 %all-to-all-start.2 = ((bf16[8,128,576]{1,2,0:T(8,128)(2,1)}), bf16[8,128,576]{1,2,0:T(8,128)(2,1)}, u32[]{:S(2)}, u32[]{:S(2)}) async-start(bf16[8,128,576]{1,2,0:T(8,128)(2,1)} %bitcast.147), calls=%async_computation.2 | async-start | bytes 2359296 | tf_op jit(solution)/shard_map/all_to_all | solution.py:123
  118.8 3.0 fusion.20
  121.9 28.7 %all-to-all-done.2 = bf16[8,128,576]{1,2,0:T(8,128)(2,1)} async-done(((bf16[8,128,576]{1,2,0:T(8,128)(2,1)}), bf16[8,128,576]{1,2,0:T(8,128)(2,1)}, u32[]{:S(2)}, u32[]{:S(2)}) %all-to-all-start.2) | async-done | bytes 1179680 | tf_op jit(solution)/shard_map/all_to_all | solution.py:123
  150.7 3.9 %fusion.16 = bf16[1,1024,768]{2,1,0:T(8,128)(2,1)} fusion(bf16[768,576]{0,1:T(8,128)(2,1)S(1)} %bitcast.144, bf16[8,128,576]{1,2,0:T(8,128)(2,1)} %all-to-all-done.2), kind=kOutput, calls=%fused_computation.31 | convolution fusion | flops 906756096 | bytes 3637248 | tf_op jit(solution)/shard_map/dot_general | solution.py:67
  154.6 0.9 copy-done.13
  155.5 1.8 fusion.15
  157.3 8.5 %copy.106 = bf16[1,1024,768]{1,0,2:T(2,128)(2,1)} copy(bf16[1,1024,768]{2,1,0:T(8,128)(2,1)} %fusion.15) | data formatting | bytes 3145728
  165.8 3.7 %copy.133 = bf16[768,1,1024]{2,0,1:T(8,128)(2,1)} copy(bf16[768,1,1024]{2,1,0:T(2,128)(2,1)} %bitcast.145) | data formatting | bytes 3145728
  169.8 1.5 copy_bitcast_fusion.1
  171.3 3.3 %fusion.4 = f32[768,3,192]{2,0,1:T(8,128)} fusion(bf16[3,192,1024]{2,1,0:T(8,128)(2,1)S(1)} %bitcast.152, f32[768]{0:T(1024)S(1)} %copy-done.17, bf16[1,1024,768]{2,1,0:T(8,128)(2,1)S(1)} %copy-done.1, f32[1024]{0:T(1024)S(1)} %add_rsqrt_fusion, f32[1024]{0:T(1024)S(1)} %broadcast_multiply_fusion.2), kind=kOutput, calls=%fused_computation.16 | convolution fusion | flops 909901824 | bytes 4533248 | tf_op jit(solution)/shard_map/dot_general | solution.py:57
  174.6 1.9 convert_element_type.92
  176.6 14.7 %reduce-scatter.12.cloned.1.call-done = f32[96,192]{1,0:T(8,128)} async-done(((f32[768,192]{1,0:T(8,128)}), f32[96,192]{1,0:T(8,128)}) %reduce-scatter.12.cloned.1.call-update) | async-done | bytes 73744
  191.3 1.6 copy.109
  192.9 3.7 %all-reduce.5.cloned.1.call-done = bf16[1,1024,768]{2,1,0:T(8,128)(2,1)} async-done(((bf16[1,1024,768]{2,1,0:T(8,128)(2,1)}), bf16[1,1024,768]{2,1,0:T(8,128)(2,1)}) %all-reduce.5.cloned.1.call-update) | async-done | bytes 1572880 | tf_op jit(solution)/shard_map/psum | solution.py:126
  196.6 1.8 convert_element_type.118
  198.7 1.2 multiply_reduce_fusion.2
  199.9 2.5 multiply_reduce_fusion.3
  202.4 0.9 copy.101
  203.3 21.7 %psum.15 = f32[192]{0:T(256)} all-reduce(f32[192]{0:T(256)S(1)} %get-tuple-element.41), channel_id=1, replica_groups=mesh['tm'=8,'tensor'=4] {'tm'}, use_global_device_ids=true, to_apply=%region_15.16 | all-reduce | flops 192 | bytes 1536 | tf_op jit(solution)/shard_map/psum | solution.py:142
  225.0 1.4 reshape_bitcast_fusion
  226.4 1.1 copy.107
  227.6 1.8 add_convert_fusion.1
  229.3 0.9 copy.100
  230.3 63.9 %reduce-scatter.8.cloned.1.call-done = f32[96,3,192]{2,0,1:T(8,128)} async-done(((f32[768,3,192]{2,0,1:T(8,128)}), f32[96,3,192]{2,0,1:T(8,128)}) %reduce-scatter.8.cloned.1.call-update) | async-done | bytes 221200 | tf_op jit(solution)/shard_map/reduce_scatter | solution.py:139
  294.2 1.6 convert_element_type.120
  (75 shorter events, 9.6 us)
Async XLA Ops:
  8.0 19.2 %copy-start = (bf16[768,3,192]{0,2,1:T(8,128)(2,1)S(1)}, bf16[768,3,192]{0,2,1:T(8,128)(2,1)}, u32[]{:S(2)}) copy-start(bf16[768,3,192]{0,2,1:T(8,128)(2,1)} %param.8) | copy-start | bytes 2654212
  11.6 14.7 %copy-start.1 = (bf16[1,1024,768]{2,1,0:T(8,128)(2,1)S(1)}, bf16[1,1024,768]{2,1,0:T(8,128)(2,1)}, u32[]{:S(2)}) copy-start(bf16[1,1024,768]{2,1,0:T(8,128)(2,1)} %param.6) | copy-start | bytes 4718596
  18.9 67.3 %all-to-all-start.1 = ((bf16[8,2,12288]{2,1,0:T(2,128)(2,1)}), bf16[8,2,12288]{2,1,0:T(2,128)(2,1)}, u32[]{:S(2)}, u32[]{:S(2)}) async-start(bf16[8,2,12288]{2,1,0:T(2,128)(2,1)} %reshape.159), calls=%async_computation.1 | async-start | bytes 786432 | tf_op jit(solution)/shard_map/all_to_all | solution.py:119
  26.2 1.0 copy-start.17
  28.5 1.0 copy-start.14
  29.5 10.9 %copy-start.16 = (s32[8,16,2]{1,2,0:T(2,128)S(1)}, s32[8,16,2]{1,2,0:T(2,128)}, u32[]{:S(2)}) copy-start(s32[8,16,2]{1,2,0:T(2,128)} %param.10) | copy-start | bytes 3076
  29.8 37.2 %collective-permute-start.6 = (bf16[1,128,576]{1,2,0:T(8,128)(2,1)S(1)}, bf16[1,128,576]{1,2,0:T(8,128)(2,1)}, u32[]{:S(2)}, u32[]{:S(2)}) collective-permute-start(bf16[1,128,576]{1,2,0:T(8,128)(2,1)S(1)} %get-tuple-element.48), channel_id=1, source_target_pairs={{0,28},{4,24},{8,20},{12,16},{16,12},{20,8},{24,4},{28,0},{1,29},{... | collective-permute-start | bytes 442376 | tf_op jit(solution)/shard_map/ppermute | solution.py:97
  34.6 30.9 %collective-permute-start.5 = (bf16[1,128,576]{1,2,0:T(8,128)(2,1)S(1)}, bf16[1,128,576]{1,2,0:T(8,128)(2,1)}, u32[]{:S(2)}, u32[]{:S(2)}) collective-permute-start(bf16[1,128,576]{1,2,0:T(8,128)(2,1)S(1)} %get-tuple-element.49), channel_id=1, source_target_pairs={{0,24},{4,28},{8,16},{12,20},{16,8},{20,12},{24,0},{28,4},{1,25},{... | collective-permute-start | bytes 442376 | tf_op jit(solution)/shard_map/ppermute | solution.py:97
  35.1 28.7 %collective-permute-start.4 = (bf16[1,128,576]{1,2,0:T(8,128)(2,1)S(1)}, bf16[1,128,576]{1,2,0:T(8,128)(2,1)}, u32[]{:S(2)}, u32[]{:S(2)}) collective-permute-start(bf16[1,128,576]{1,2,0:T(8,128)(2,1)S(1)} %get-tuple-element.50), channel_id=1, source_target_pairs={{0,20},{4,16},{8,28},{12,24},{16,4},{20,0},{24,12},{28,8},{1,21},{... | collective-permute-start | bytes 442376 | tf_op jit(solution)/shard_map/ppermute | solution.py:97
  35.7 13.5 %collective-permute-start.1 = (bf16[1,128,576]{1,2,0:T(8,128)(2,1)S(1)}, bf16[1,128,576]{1,2,0:T(8,128)(2,1)}, u32[]{:S(2)}, u32[]{:S(2)}) collective-permute-start(bf16[1,128,576]{1,2,0:T(8,128)(2,1)S(1)} %get-tuple-element.53), channel_id=1, source_target_pairs={{0,8},{4,12},{8,0},{12,4},{16,24},{20,28},{24,16},{28,20},{1,9},{5... | collective-permute-start | bytes 442376 | tf_op jit(solution)/shard_map/ppermute | solution.py:97
  38.9 5.3 %collective-permute-start = (bf16[1,128,576]{1,2,0:T(8,128)(2,1)S(1)}, bf16[1,128,576]{1,2,0:T(8,128)(2,1)}, u32[]{:S(2)}, u32[]{:S(2)}) collective-permute-start(bf16[1,128,576]{1,2,0:T(8,128)(2,1)S(1)} %get-tuple-element.54), channel_id=1, source_target_pairs={{0,4},{4,0},{8,12},{12,8},{16,20},{20,16},{24,28},{28,24},{1,5},{5... | collective-permute-start | bytes 442376 | tf_op jit(solution)/shard_map/ppermute | solution.py:97
  44.2 8.8 %collective-permute-start.2 = (bf16[1,128,576]{1,2,0:T(8,128)(2,1)S(1)}, bf16[1,128,576]{1,2,0:T(8,128)(2,1)S(1)}, u32[]{:S(2)}, u32[]{:S(2)}) collective-permute-start(bf16[1,128,576]{1,2,0:T(8,128)(2,1)S(1)} %get-tuple-element.52), channel_id=1, source_target_pairs={{0,12},{4,8},{8,4},{12,0},{16,28},{20,24},{24,20},{28,16},{1,13},{... | collective-permute-start | bytes 442376 | tf_op jit(solution)/shard_map/ppermute | solution.py:97
  49.2 14.0 %collective-permute-start.3 = (bf16[1,128,576]{1,2,0:T(8,128)(2,1)S(1)}, bf16[1,128,576]{1,2,0:T(8,128)(2,1)S(1)}, u32[]{:S(2)}, u32[]{:S(2)}) collective-permute-start(bf16[1,128,576]{1,2,0:T(8,128)(2,1)S(1)} %get-tuple-element.51), channel_id=1, source_target_pairs={{0,16},{4,20},{8,24},{12,28},{16,0},{20,4},{24,8},{28,12},{1,17},{... | collective-permute-start | bytes 442376 | tf_op jit(solution)/shard_map/ppermute | solution.py:97
  72.3 4.5 %copy-start.5 = (bf16[8,128,1,3,64]{4,0,3,1,2:T(8,128)(2,1)}, bf16[8,128,1,3,64]{4,0,3,1,2:T(8,128)(2,1)S(1)}, u32[]{:S(2)}) copy-start(bf16[8,128,1,3,64]{4,0,3,1,2:T(8,128)(2,1)S(1)} %copy.114) | copy-start | bytes 1179652
  76.8 1.2 copy-start.2
  76.8 3.2 %copy-start.10 = (f32[128,3,8]{2,1,0:T(4,128)}, f32[128,3,8]{2,1,0:T(4,128)S(1)}, u32[]{:S(2)}) copy-start(f32[128,3,8]{2,1,0:T(4,128)S(1)} %get-tuple-element.59) | copy-start | bytes 36868
  76.8 1.9 copy-start.12
  78.7 6.8 %copy-start.8 = (f32[128,3,8]{2,1,0:T(4,128)}, f32[128,3,8]{2,1,0:T(4,128)S(1)}, u32[]{:S(2)}) copy-start(f32[128,3,8]{2,1,0:T(4,128)S(1)} %fusion.29) | copy-start | bytes 36868
  91.4 7.6 %copy-start.11 = (f32[128,3,8]{2,1,0:T(4,128)S(1)}, f32[128,3,8]{2,1,0:T(4,128)}, u32[]{:S(2)}) copy-start(f32[128,3,8]{2,1,0:T(4,128)} %copy-done.10) | copy-start | bytes 36868
  93.4 19.3 %all-to-all-start = ((bf16[8,128,192]{1,2,0:T(8,128)(2,1)}), bf16[8,128,192]{1,2,0:T(8,128)(2,1)S(1)}, u32[]{:S(2)}, u32[]{:S(2)}) async-start(bf16[8,128,192]{1,2,0:T(8,128)(2,1)} %bitcast.18), calls=%async_computation | async-start | bytes 786432 | tf_op jit(solution)/shard_map/all_to_all | solution.py:106
  99.0 3.8 %copy-start.3 = (f32[128,3,8,8]{2,3,1,0:T(8,128)S(1)}, f32[128,3,8,8]{2,3,1,0:T(8,128)}, u32[]{:S(2)}) copy-start(f32[128,3,8,8]{2,3,1,0:T(8,128)} %copy-done.2) | copy-start | bytes 294916
  99.0 3.8 %copy-start.9 = (f32[128,3,8]{2,1,0:T(4,128)S(1)}, f32[128,3,8]{2,1,0:T(4,128)}, u32[]{:S(2)}) copy-start(f32[128,3,8]{2,1,0:T(4,128)} %copy-done.8) | copy-start | bytes 36868
  102.8 1.1 copy-start.7
  103.9 1.1 copy-start.6
  105.1 1.1 copy-start.15
  112.8 37.9 %all-to-all-start.2 = ((bf16[8,128,576]{1,2,0:T(8,128)(2,1)}), bf16[8,128,576]{1,2,0:T(8,128)(2,1)}, u32[]{:S(2)}, u32[]{:S(2)}) async-start(bf16[8,128,576]{1,2,0:T(8,128)(2,1)} %bitcast.147), calls=%async_computation.2 | async-start | bytes 2359296 | tf_op jit(solution)/shard_map/all_to_all | solution.py:123
  118.8 72.5 %reduce-scatter.12.cloned.1.call-start = ((), (), s32[]{:S(2)}) async-start(), calls=%async_computation.9 | async-start | bytes 884736
  121.9 74.8 %all-reduce.5.cloned.1.call-start = ((), (), s32[]{:S(2)}) async-start(), calls=%async_computation.6 | async-start | bytes 3145728 | tf_op jit(solution)/shard_map/psum | solution.py:126
  154.6 1.0 copy-start.13
  154.6 70.4 %reduce-scatter.10.cloned.1.call-start = ((), (), s32[]{:S(2)}) async-start(), calls=%async_computation.8 | async-start | bytes 1966080
  169.5 124.7 %reduce-scatter.8.cloned.1.call-start = ((), (), s32[]{:S(2)}) async-start(), calls=%async_computation.7 | async-start | bytes 2654208 | tf_op jit(solution)/shard_map/reduce_scatter | solution.py:139
  196.6 2.1 copy-start.4
Sparse Core Ops, SparseCore 0:
  122.9 68.3 reduce-scatter.11
  193.8 27.0 reduce-scatter.9
  224.4 69.7 reduce-scatter.7
Sparse Core Ops, SparseCore 1:
  154.7 41.9 all-reduce.4
